TPU v7x, 256 devices: a whole 4x4x8 slice. The times are simulated.
256 devices in a mesh: section: 4 (over x), tp: 64 (over y, z, core).
Axes of the slice: x: 4, y: 4, z: 8, core: 2. Of those that a mesh axis runs over, the one named last changes fastest.
Arguments:
- tokens: bfloat16 [64, 8192], P(None, 'tp'), may hold values from -6 to 6
- norm_gain: float32 [4, 8192], P('section'), may hold values from 0.1 to 1.9
- gate_weight: bfloat16 [4, 8192, 16384], P('section', None, 'tp'), may hold values from -0.09375 to 0.09375
- up_weight: bfloat16 [4, 8192, 16384], P('section', None, 'tp'), may hold values from -0.09375 to 0.09375
- gate_mask: int32 [4, 128, 256], P('section', None, 'tp'), may hold values 0 or 1
- up_mask: int32 [4, 128, 256], P('section', None, 'tp'), may hold values 0 or 1
- down_weight: bfloat16 [4, 16384, 8192], P('section', 'tp'), may hold values from -0.125 to 0.125
- down_mask: int32 [4, 256, 128], P('section', 'tp'), may hold values 0 or 1
- slot_order: int32 [4, 256], P('section', 'tp'), may hold values from 0 to 255, as said below
Outputs:
- received: bfloat16 [4, 64, 8192], P('section', None, 'tp')
Inputs may be any that keep to these rules, and one draw needn't show every extreme that they name: `slot_order`: for each section a permutation of the 256 hidden blocks. Slot k lies on tp device k // 4; block b is computed on tp device b // 4. The slots of tp device t take exactly 1 block from each of the tp devices t, t + 1, ..., t + 4 - 1 (mod 64) and none from others. `gate_mask`: 1 keeps a block, 0 prunes it. `up_mask`: 1 keeps a block, 0 prunes it. `down_mask`: 1 keeps a block, 0 prunes it.
All inputs are finite; a program needn't handle non-finite values.
Results may differ from a plain program's by a relative error of at most 0.014.
Values may be sent and summed in bfloat16 or wider, within the bound.
A program may use at most 128 MiB of HBM per device.

v0:
```python
import jax
import jax.numpy as jnp
from jax import lax
from jax.sharding import PartitionSpec as P


def passed_along(block, axis, distance):
    devices = range(lax.axis_size(axis))
    route = [((i - distance) % len(devices), i) for i in devices]
    return lax.ppermute(block, axis, route)


def expand_mask(mask, width):
    return jnp.repeat(jnp.repeat(mask, width, axis=0), width, axis=1)


def masked(weight, mask, width):
    return weight * expand_mask(mask, width).astype(jnp.bfloat16)


def body(
    tokens,
    norm_gain,
    gate_weight,
    up_weight,
    gate_mask,
    up_mask,
    down_weight,
    down_mask,
    slot_order,
):
    sections = lax.axis_size("section")
    tp_count = lax.axis_size("tp")
    section_pos = lax.axis_index("section")
    tp_pos = lax.axis_index("tp")
    width = gate_weight.shape[1] // gate_mask.shape[1]
    w_gate = masked(gate_weight[0], gate_mask[0], width)
    w_up = masked(up_weight[0], up_mask[0], width)
    w_down = masked(down_weight[0], down_mask[0], width)
    gain = norm_gain[0]
    my_blocks = slot_order[0]
    per_device = my_blocks.shape[0]
    row_count, own_cols = tokens.shape
    window = min(tp_count, per_device)
    capacity = per_device // window
    slot_ids = jnp.arange(capacity, dtype=jnp.int32)
    my_source = my_blocks // per_device
    my_offset = (my_source - tp_pos) % tp_count
    lanes = jnp.arange(per_device, dtype=jnp.int32)
    earlier = (my_source[None, :] == my_source[:, None]) & (lanes[None, :] < lanes[:, None])
    my_rank = jnp.sum(earlier.astype(jnp.int32), axis=1)
    send_lists = []
    for offset in range(window):
        if offset == 0:
            table_row = my_blocks
        else:
            table_row = passed_along(my_blocks, "tp", offset)
        row_source = table_row // per_device
        row_block = table_row % per_device
        from_me = (row_source == tp_pos).astype(jnp.int32)
        order_rank = jnp.cumsum(from_me) - 1
        picks = (from_me[None, :] == 1) & (order_rank[None, :] == slot_ids[:, None])
        send_lists.append(jnp.sum(jnp.where(picks, row_block[None, :], 0), axis=1))
    x_full = lax.all_gather(tokens, "tp", axis=1, tiled=True)
    saved = jnp.zeros((row_count, own_cols), jnp.bfloat16)
    for round_pos in range(sections):
        x_own = lax.dynamic_slice_in_dim(x_full, tp_pos * own_cols, own_cols, 1)
        widened = x_full.astype(jnp.float32)
        scale = lax.rsqrt(jnp.mean(widened * widened, axis=-1, keepdims=True) + 1e-05)
        normed = (widened * scale * gain).astype(jnp.bfloat16)
        gate = jnp.dot(normed, w_gate, preferred_element_type=jnp.float32)
        upper = jnp.dot(normed, w_up, preferred_element_type=jnp.float32)
        hidden = (jax.nn.silu(gate) * upper).astype(jnp.bfloat16)
        flat = (
            hidden.reshape(row_count, per_device, width)
            .transpose(1, 0, 2)
            .reshape(per_device, row_count * width)
        )
        arrivals = []
        for gather_offset in range(window):
            outgoing = flat[send_lists[gather_offset]]
            if gather_offset == 0:
                arrivals.append(outgoing)
            else:
                arrivals.append(passed_along(outgoing, "tp", tp_count - gather_offset))
        stacked = jnp.stack(arrivals)
        chosen = stacked[my_offset, my_rank]
        mine = (
            chosen.reshape(per_device, row_count, width)
            .transpose(1, 0, 2)
            .reshape(row_count, per_device * width)
        )
        partial_sum = jnp.dot(mine, w_down, preferred_element_type=jnp.float32)
        summed = lax.psum_scatter(partial_sum, "tp", scatter_dimension=1, tiled=True)
        y_own = (x_own.astype(jnp.float32) + summed).astype(jnp.bfloat16)
        section_full = lax.all_gather(y_own, "tp", axis=1, tiled=True)
        x_full = passed_along(section_full, "section", 1)
        got_own = lax.dynamic_slice_in_dim(x_full, tp_pos * own_cols, own_cols, 1)
        saved = jnp.where(section_pos == (round_pos + 1) % sections, got_own, saved)
    return saved[None]


def solution(mesh):
    return jax.shard_map(
        body,
        mesh=mesh,
        in_specs=(
            P(None, "tp"),
            P("section", None),
            P("section", None, "tp"),
            P("section", None, "tp"),
            P("section", None, "tp"),
            P("section", None, "tp"),
            P("section", "tp", None),
            P("section", "tp", None),
            P("section", "tp"),
        ),
        out_specs=P("section", None, "tp"),
        check_vma=False,
    )
```

profile of v0, /device:TPU:1, one launch (start us, length us, event | category | flops | bytes accessed | tf_op | source)
XLA Modules:
  0.0 1125.9 jit_solution(15061843299415078217)
XLA Ops:
  6.5 3.0 collective-permute-start
  16.4 6.4 copy.36
  23.1 6.4 copy.37
  30.5 4.6 bitcast_multiply_fusion.2
  46.1 38.5 %all-gather.6.cloned.1.call-done = bf16[64,8192]{1,0:T(8,128)(2,1)} async-done(((bf16[64,128]{1,0:T(8,128)(2,1)}), bf16[64,8192]{1,0:T(8,128)(2,1)}) %all-gather.6.cloned.1.call-update) | async-done | bytes 1048592 | tf_op jit(solution)/shard_map/all_gather | solution.py:64
  86.2 4.1 fusion.34
  92.3 4.3 collective-permute-start.3
  98.5 6.4 copy.41
  105.0 4.4 bitcast_multiply_fusion
  110.6 4.9 fusion.6
  115.6 130.5 %reduce-scatter.5.cloned.1.call-done = f32[64,128]{1,0:T(8,128)} async-done(((f32[64,8192]{1,0:T(8,128)}), f32[64,128]{1,0:T(8,128)}) %reduce-scatter.5.cloned.1.call-update) | async-done | bytes 32784 | tf_op jit(solution)/shard_map/reduce_scatter | solution.py:94
  247.5 76.0 %all-gather.8.cloned.1.call-done = bf16[64,8192]{1,0:T(8,128)(2,1)} async-done(((bf16[64,128]{1,0:T(8,128)(2,1)}), bf16[64,8192]{1,0:T(8,128)(2,1)}) %all-gather.8.cloned.1.call-update) | async-done | bytes 1048592 | tf_op jit(solution)/shard_map/all_gather | solution.py:96
  324.5 24.8 %collective-permute-done.6 = bf16[64,8192]{1,0:T(8,128)(2,1)S(1)} collective-permute-done((bf16[64,8192]{1,0:T(8,128)(2,1)}, bf16[64,8192]{1,0:T(8,128)(2,1)S(1)}, u32[]{:S(2)}, u32[]{:S(2)}) %collective-permute-start.6) | collective-permute-done | bytes 1048608 | tf_op jit(solution)/shard_map/ppermute | solution.py:10
  349.7 3.7 fusion.31
  356.4 4.3 collective-permute-start.8
  361.7 3.0 collective-permute-done.9
  365.8 4.9 fusion.4
  370.8 132.0 %reduce-scatter.7.cloned.1.call-done = f32[64,128]{1,0:T(8,128)} async-done(((f32[64,8192]{1,0:T(8,128)}), f32[64,128]{1,0:T(8,128)}) %reduce-scatter.7.cloned.1.call-update) | async-done | bytes 32784 | tf_op jit(solution)/shard_map/reduce_scatter | solution.py:94
  504.2 75.2 %all-gather.10.cloned.1.call-done = bf16[64,8192]{1,0:T(8,128)(2,1)} async-done(((bf16[64,128]{1,0:T(8,128)(2,1)}), bf16[64,8192]{1,0:T(8,128)(2,1)}) %all-gather.10.cloned.1.call-update) | async-done | bytes 1048592 | tf_op jit(solution)/shard_map/all_gather | solution.py:96
  580.5 24.8 %collective-permute-done.10 = bf16[64,8192]{1,0:T(8,128)(2,1)S(1)} collective-permute-done((bf16[64,8192]{1,0:T(8,128)(2,1)}, bf16[64,8192]{1,0:T(8,128)(2,1)S(1)}, u32[]{:S(2)}, u32[]{:S(2)}) %collective-permute-start.10) | collective-permute-done | bytes 1048608 | tf_op jit(solution)/shard_map/ppermute | solution.py:10
  605.7 3.7 fusion.27
  612.3 4.3 collective-permute-start.12
  621.8 4.9 fusion.2
  626.8 132.0 %reduce-scatter.9.cloned.1.call-done = f32[64,128]{1,0:T(8,128)} async-done(((f32[64,8192]{1,0:T(8,128)}), f32[64,128]{1,0:T(8,128)}) %reduce-scatter.9.cloned.1.call-update) | async-done | bytes 32784 | tf_op jit(solution)/shard_map/reduce_scatter | solution.py:94
  760.2 75.6 %all-gather.12.cloned.1.call-done = bf16[64,8192]{1,0:T(8,128)(2,1)} async-done(((bf16[64,128]{1,0:T(8,128)(2,1)}), bf16[64,8192]{1,0:T(8,128)(2,1)}) %all-gather.12.cloned.1.call-update) | async-done | bytes 1048592 | tf_op jit(solution)/shard_map/all_gather | solution.py:96
  837.0 24.8 %collective-permute-done.14 = bf16[64,8192]{1,0:T(8,128)(2,1)S(1)} collective-permute-done((bf16[64,8192]{1,0:T(8,128)(2,1)}, bf16[64,8192]{1,0:T(8,128)(2,1)S(1)}, u32[]{:S(2)}, u32[]{:S(2)}) %collective-permute-start.14) | collective-permute-done | bytes 1048608 | tf_op jit(solution)/shard_map/ppermute | solution.py:10
  862.1 3.7 fusion.23
  868.8 4.3 collective-permute-start.16
  878.2 4.9 fusion
  883.2 132.0 %reduce-scatter.11.cloned.1.call-done = f32[64,128]{1,0:T(8,128)} async-done(((f32[64,8192]{1,0:T(8,128)}), f32[64,128]{1,0:T(8,128)}) %reduce-scatter.11.cloned.1.call-update) | async-done | bytes 32784 | tf_op jit(solution)/shard_map/reduce_scatter | solution.py:94
  1016.6 75.4 %all-gather.14.cloned.1.call-done = bf16[64,8192]{1,0:T(8,128)(2,1)} async-done(((bf16[64,128]{1,0:T(8,128)(2,1)}), bf16[64,8192]{1,0:T(8,128)(2,1)}) %all-gather.14.cloned.1.call-update) | async-done | bytes 1048592 | tf_op jit(solution)/shard_map/all_gather | solution.py:96
  1093.1 24.9 %collective-permute-done.18 = bf16[64,8192]{1,0:T(8,128)(2,1)} collective-permute-done((bf16[64,8192]{1,0:T(8,128)(2,1)}, bf16[64,8192]{1,0:T(8,128)(2,1)}, u32[]{:S(2)}, u32[]{:S(2)}) %collective-permute-start.18) | collective-permute-done | bytes 1048608 | tf_op jit(solution)/shard_map/ppermute | solution.py:10
  (146 shorter events, 51.5 us)
Async XLA Ops:
  6.5 78.0 %all-gather.6.cloned.1.call-start = ((), (), s32[]{:S(2)}) async-start(), calls=%async_computation.4 | async-start | bytes 1064960 | tf_op jit(solution)/shard_map/all_gather | solution.py:64
  6.5 31.1 %collective-permute-start = (s32[4]{0:T(128)}, s32[4]{0:T(128)S(1)}, u32[]{:S(2)}, u32[]{:S(2)}) collective-permute-start(s32[4]{0:T(128)} %bitcast.171), channel_id=1, source_target_pairs={{63,0},{0,1},{1,2},{2,3},{3,4},{4,5},{5,6},{6,7},{7,8},{8,9},{9,10... | collective-permute-start | bytes 56 | tf_op jit(solution)/shard_map/ppermute | solution.py:10
  9.6 30.2 %collective-permute-start.2 = (s32[4]{0:T(128)}, s32[4]{0:T(128)S(1)}, u32[]{:S(2)}, u32[]{:S(2)}) collective-permute-start(s32[4]{0:T(128)} %bitcast.172), channel_id=1, source_target_pairs={{62,0},{63,1},{0,2},{1,3},{2,4},{3,5},{4,6},{5,7},{6,8},{7,9},{8,1... | collective-permute-start | bytes 56 | tf_op jit(solution)/shard_map/ppermute | solution.py:10
  11.2 30.8 %collective-permute-start.4 = (s32[4]{0:T(128)}, s32[4]{0:T(128)S(1)}, u32[]{:S(2)}, u32[]{:S(2)}) collective-permute-start(s32[4]{0:T(128)} %bitcast.173), channel_id=1, source_target_pairs={{61,0},{62,1},{63,2},{0,3},{1,4},{2,5},{3,6},{4,7},{5,8},{6,9},{7,... | collective-permute-start | bytes 56 | tf_op jit(solution)/shard_map/ppermute | solution.py:10
  12.9 233.1 %reduce-scatter.5.cloned.1.call-start = ((), (), s32[]{:S(2)}) async-start(), calls=%async_computation.5 | async-start | bytes 2129920 | tf_op jit(solution)/shard_map/reduce_scatter | solution.py:94
  16.4 6.4 copy-start.8
  23.1 6.4 copy-start.9
  30.5 4.6 copy-start.4
  35.1 51.0 %copy-start.6 = (f32[1,8192]{1,0:T(1,128)S(1)}, f32[1,8192]{1,0:T(1,128)}, u32[]{:S(2)}) copy-start(f32[1,8192]{1,0:T(1,128)} %param.10) | copy-start | bytes 98308
  92.0 17.5 %collective-permute-start.1 = (bf16[1,4096]{1,0:T(2,128)(2,1)S(1)}, bf16[1,4096]{1,0:T(2,128)(2,1)S(1)}, u32[]{:S(2)}, u32[]{:S(2)}) collective-permute-start(bf16[1,4096]{1,0:T(2,128)(2,1)S(1)} %get-tuple-element.198), channel_id=1, source_target_pairs={{1,0},{2,1},{3,2},{4,3},{5,4},{6,5},{7,6},{8,7},{9,8},{10,9},{11,1... | collective-permute-start | bytes 24584 | tf_op jit(solution)/shard_map/ppermute | solution.py:10
  92.3 17.2 %collective-permute-start.3 = (bf16[1,4096]{1,0:T(2,128)(2,1)S(1)}, bf16[1,4096]{1,0:T(2,128)(2,1)S(1)}, u32[]{:S(2)}, u32[]{:S(2)}) collective-permute-start(bf16[1,4096]{1,0:T(2,128)(2,1)S(1)} %get-tuple-element.197), channel_id=1, source_target_pairs={{2,0},{3,1},{4,2},{5,3},{6,4},{7,5},{8,6},{9,7},{10,8},{11,9},{12,... | collective-permute-start | bytes 24584 | tf_op jit(solution)/shard_map/ppermute | solution.py:10
  96.6 12.9 %collective-permute-start.5 = (bf16[1,4096]{1,0:T(2,128)(2,1)S(1)}, bf16[1,4096]{1,0:T(2,128)(2,1)S(1)}, u32[]{:S(2)}, u32[]{:S(2)}) collective-permute-start(bf16[1,4096]{1,0:T(2,128)(2,1)S(1)} %get-tuple-element.196), channel_id=1, source_target_pairs={{3,0},{4,1},{5,2},{6,3},{7,4},{8,5},{9,6},{10,7},{11,8},{12,9},{13... | collective-permute-start | bytes 24584 | tf_op jit(solution)/shard_map/ppermute | solution.py:10
  115.5 207.9 %all-gather.8.cloned.1.call-start = ((), (), s32[]{:S(2)}) async-start(), calls=%async_computation.6 | async-start | bytes 1064960 | tf_op jit(solution)/shard_map/all_gather | solution.py:96
  247.4 255.4 %reduce-scatter.7.cloned.1.call-start = ((), (), s32[]{:S(2)}) async-start(), calls=%async_computation.7 | async-start | bytes 2129920 | tf_op jit(solution)/shard_map/reduce_scatter | solution.py:94
  323.4 25.9 %collective-permute-start.6 = (bf16[64,8192]{1,0:T(8,128)(2,1)}, bf16[64,8192]{1,0:T(8,128)(2,1)S(1)}, u32[]{:S(2)}, u32[]{:S(2)}) collective-permute-start(bf16[64,8192]{1,0:T(8,128)(2,1)} %all-gather.8.cloned.1.call-done), channel_id=1, source_target_pairs={{192,0},{0,64},{64,128},{128,192},{193,1},{1,65},{65,129},{129,193... | collective-permute-start | bytes 3145736 | tf_op jit(solution)/shard_map/ppermute | solution.py:10
  355.2 6.5 collective-permute-start.7
  356.4 5.4 collective-permute-start.8
  360.7 4.1 collective-permute-start.9
  370.7 208.7 %all-gather.10.cloned.1.call-start = ((), (), s32[]{:S(2)}) async-start(), calls=%async_computation.8 | async-start | bytes 1064960 | tf_op jit(solution)/shard_map/all_gather | solution.py:96
  504.2 254.6 %reduce-scatter.9.cloned.1.call-start = ((), (), s32[]{:S(2)}) async-start(), calls=%async_computation.9 | async-start | bytes 2129920 | tf_op jit(solution)/shard_map/reduce_scatter | solution.py:94
  579.4 25.9 %collective-permute-start.10 = (bf16[64,8192]{1,0:T(8,128)(2,1)}, bf16[64,8192]{1,0:T(8,128)(2,1)S(1)}, u32[]{:S(2)}, u32[]{:S(2)}) collective-permute-start(bf16[64,8192]{1,0:T(8,128)(2,1)} %all-gather.10.cloned.1.call-done), channel_id=1, source_target_pairs={{192,0},{0,64},{64,128},{128,192},{193,1},{1,65},{65,129},{129,193... | collective-permute-start | bytes 3145736 | tf_op jit(solution)/shard_map/ppermute | solution.py:10
  611.2 6.5 collective-permute-start.11
  612.3 5.4 collective-permute-start.12
  616.6 4.1 collective-permute-start.13
  626.7 209.2 %all-gather.12.cloned.1.call-start = ((), (), s32[]{:S(2)}) async-start(), calls=%async_computation.10 | async-start | bytes 1064960 | tf_op jit(solution)/shard_map/all_gather | solution.py:96
  760.2 255.0 %reduce-scatter.11.cloned.1.call-start = ((), (), s32[]{:S(2)}) async-start(), calls=%async_computation.11 | async-start | bytes 2129920 | tf_op jit(solution)/shard_map/reduce_scatter | solution.py:94
  835.9 25.9 %collective-permute-start.14 = (bf16[64,8192]{1,0:T(8,128)(2,1)}, bf16[64,8192]{1,0:T(8,128)(2,1)S(1)}, u32[]{:S(2)}, u32[]{:S(2)}) collective-permute-start(bf16[64,8192]{1,0:T(8,128)(2,1)} %all-gather.12.cloned.1.call-done), channel_id=1, source_target_pairs={{192,0},{0,64},{64,128},{128,192},{193,1},{1,65},{65,129},{129,193... | collective-permute-start | bytes 3145736 | tf_op jit(solution)/shard_map/ppermute | solution.py:10
  867.6 6.5 collective-permute-start.15
  868.8 5.4 collective-permute-start.16
  873.1 4.1 collective-permute-start.17
  883.2 208.8 %all-gather.14.cloned.1.call-start = ((), (), s32[]{:S(2)}) async-start(), calls=%async_computation.12 | async-start | bytes 1064960 | tf_op jit(solution)/shard_map/all_gather | solution.py:96
  1092.0 26.0 %collective-permute-start.18 = (bf16[64,8192]{1,0:T(8,128)(2,1)}, bf16[64,8192]{1,0:T(8,128)(2,1)}, u32[]{:S(2)}, u32[]{:S(2)}) collective-permute-start(bf16[64,8192]{1,0:T(8,128)(2,1)} %all-gather.14.cloned.1.call-done), channel_id=1, source_target_pairs={{192,0},{0,64},{64,128},{128,192},{193,1},{1,65},{65,129},{129,193... | collective-permute-start | bytes 3145736 | tf_op jit(solution)/shard_map/ppermute | solution.py:10
  (7 other events, 24.2 us)
Sparse Core Ops, SparseCore 0:
  13.0 71.5 all-gather.5
  115.6 130.3 reduce-scatter.4
  248.9 74.4 all-gather.7
  370.9 131.9 reduce-scatter.6
  505.2 74.1 all-gather.9
  626.8 131.9 reduce-scatter.8
  761.7 74.1 all-gather.11
  883.3 131.9 reduce-scatter.10
  1017.8 74.1 all-gather.13
where the time goes:
time: 1130 us
  waiting for transfers between devices  976 us (86%)
  matrix products  40.5 us (4%)
  starting transfers between devices  37.1 us (3%)
  other arithmetic  25.9 us (2%)
  local copies, waits for them, and re-layouts  25.1 us (2%)
  between operations  21.4 us (2%)
    reduce_scatter x4, waiting for transfers between devices, body(): lax.psum_scatter(partial_sum, 'tp', scatter_dimension=1, tiled=True)  527 us
    all_gather x4, waiting for transfers between devices, body(): section_full = lax.all_gather(y_own, 'tp', axis=1, tiled=True)  302 us
    ppermute x19, waiting for transfers between devices, passed_along(): return lax.ppermute(block, axis, route)  108 us
    all_gather x1, waiting for transfers between devices, body(): x_full = lax.all_gather(tokens, 'tp', axis=1, tiled=True)  38.5 us
    ppermute x19, starting transfers between devices, passed_along(): return lax.ppermute(block, axis, route)  36.8 us
  transfers between devices with their start and end apart: 28, of which 16 were waited for; matrix products, arithmetic and copies ran while one was open for 3% of the time, Pallas kernels for 0%

commit v1 on v0

v1 whole, which is shorter than its diff:
```python
import functools

import jax
import jax.numpy as jnp
from jax import lax
from jax.experimental import pallas as pl
from jax.experimental.pallas import tpu as pltpu
from jax.sharding import PartitionSpec as P

MESH = pl.DeviceIdType.MESH
BF = jnp.bfloat16
F32 = jnp.float32
REACH = 4
GROUP = 4


def tp_grid(count):
    ny = {64: 4, 32: 4, 16: 2, 8: 2}[count]
    return ny, count // (2 * ny)


def kernel(
    sections,
    ny,
    nz,
    tokens_h,
    gain_h,
    wg_h,
    wu_h,
    gm_h,
    um_h,
    wd_h,
    dm_h,
    so_h,
    out_ref,
    wg,
    wu,
    wd,
    wdp,
    gain,
    gm,
    um,
    dm,
    so_v,
    gme,
    ume,
    perm,
    xbuf,
    xprev,
    hsend,
    hrecv,
    part,
    psend,
    precv,
    ysend,
    yrecv,
    zsend,
    zrecv,
    lsem,
    so_ss,
    so_rs,
    az_ss,
    az_rs,
    ay_ss,
    ay_rs,
    ap_ss,
    ap_rs,
    h_ss,
    h_rs,
    p_ss,
    p_rs,
    y_ss,
    y_rs,
    z_ss,
    z_rs,
    x_ss,
    x_rs,
):
    nt = ny * nz * 2
    rows = tokens_h.shape[0]
    feats = nt * 128
    groups = nz // GROUP
    s = lax.axis_index("section")
    t = lax.axis_index("tp")
    c = t % 2
    chip = t // 2
    z = chip % nz
    y = chip // nz
    s_next = (s + 1) % sections
    s_last = (s + sections - 1) % sections
    far = [nz // 2 + p // 2 if p % 2 == 0 else nz // 2 - 1 - p // 2 for p in range(nz)]
    near = far[::-1]
    y_far = [ny // 2] + [d for d in range(1, ny) if d != ny // 2]

    def pos(yy, zz):
        return (yy % ny) * nz + zz % nz

    def tp_of(yy, zz, cc):
        return pos(yy, zz) * 2 + cc

    partner = t + 1 - 2 * c

    def remote(src, dst, ss, rs, sec, tp):
        return pltpu.make_async_remote_copy(
            src_ref=src,
            dst_ref=dst,
            send_sem=ss,
            recv_sem=rs,
            device_id=(sec, tp),
            device_id_type=MESH,
        )

    loads = [
        pltpu.make_async_copy(src, dst, lsem.at[i])
        for i, (src, dst) in enumerate(
            [
                (so_h, so_v.at[0]),
                (gm_h, gm),
                (um_h, um),
                (dm_h, dm),
                (gain_h, gain),
                (wg_h, wg),
                (wu_h, wu),
                (wd_h, wd),
            ]
        )
    ]
    for one in loads:
        one.start()
    token_load = pltpu.make_async_copy(tokens_h, xbuf.at[0, 0, c], lsem.at[9])

    @pl.when(s == 0)
    def _():
        token_load.start()

    barrier = pltpu.get_barrier_semaphore()
    peers = [(s, partner)]
    peers += [(s, tp_of(y + d, z, c)) for d in range(1, ny)]
    peers += [(s, tp_of(y, z + d, c)) for d in range(1, nz)]
    peers += [(s, (t + d) % nt) for d in range(1, REACH)]
    peers += [(s, (t + nt - d) % nt) for d in range(1, REACH)]
    peers += [(s_next, tp_of(y, z + d, c)) for d in range(nz)]
    peers += [(s_last, tp_of(y, z + d, c)) for d in range(nz)]
    for peer in peers:
        pl.semaphore_signal(barrier, inc=1, device_id=peer, device_id_type=MESH)
    pl.semaphore_wait(barrier, len(peers))

    for one in loads[:5]:
        one.wait()
    so_copies = [
        remote(so_v.at[0], so_v.at[j], so_ss.at[j], so_rs.at[j], s, (t + j) % nt)
        for j in range(1, REACH)
    ]
    for one in so_copies:
        one.start()

    own = xbuf.at[0, 0, c]

    def z_gather(d):
        return remote(
            own, xbuf.at[0, d, c], az_ss.at[d], az_rs.at[d], s, tp_of(y, z + d, c)
        )

    def y_gather(dy, d):
        return remote(
            xbuf.at[0, d, c],
            xbuf.at[dy, d, c],
            ay_ss.at[dy, d],
            ay_rs.at[dy, d],
            s,
            tp_of(y + dy, z, c),
        )

    def p_gather(dy, d):
        return remote(
            xbuf.at[dy, d, c],
            xbuf.at[dy, d, c],
            ap_ss.at[dy, d],
            ap_rs.at[dy, d],
            s,
            partner,
        )

    keep_copy = remote(own, xprev, x_ss.at[0], x_rs.at[0], s_next, t)

    def z_scatter(p):
        return remote(
            zsend.at[p],
            zrecv.at[p],
            z_ss.at[p],
            z_rs.at[p],
            s_next,
            tp_of(y, z + far[p], c),
        )

    def send_own():
        for d in far[:-1]:
            z_gather(d).start()
        for dy in y_far:
            y_gather(dy, 0).start()
        p_gather(0, 0).start()
        keep_copy.start()

    def arrive():
        keep_copy.wait_recv()
        total = xprev[...].astype(F32)
        for p in range(nz):
            z_scatter(p).wait_recv()
            total = total + zrecv[p].astype(F32)
        return total.astype(BF)

    @pl.when(s == 0)
    def _():
        token_load.wait()
        send_own()

    spread_at = lax.broadcasted_iota(jnp.int32, (4, 256), 1) // 64
    spread_of = lax.broadcasted_iota(jnp.int32, (4, 256), 0)
    spread = jnp.where(spread_at == spread_of, 1.0, 0.0).astype(BF)
    for raw, wide in ((gm, gme), (um, ume)):
        wide[...] = lax.dot_general(
            raw[...].astype(BF),
            spread,
            (((0,), (0,)), ((), ())),
            preferred_element_type=F32,
        )

    def mask_up(weight, wide):
        @pl.loop(0, feats // 64)
        def _(i):
            at = pl.ds(pl.multiple_of(i * 64, 64), 64)
            row = jnp.broadcast_to(wide[pl.ds(i, 1), :], (16, 256)).astype(BF)
            block = weight[at, :].reshape(4, 16, 256) * row[None]
            weight[at, :] = block.reshape(64, 256)

    loads[5].wait()
    mask_up(wg, gme)
    loads[6].wait()
    mask_up(wu, ume)

    down_bits = dm[...].astype(BF)
    pick_row = lax.broadcasted_iota(jnp.int32, (feats // 64, 256), 0)
    pick_lane = lax.broadcasted_iota(jnp.int32, (feats // 64, 256), 1) // 64
    sort_row = lax.broadcasted_iota(jnp.int32, (256, 256), 0)
    sort_lane = lax.broadcasted_iota(jnp.int32, (256, 256), 1)
    sender = (so_v[0] // 4 + nt - t) % nt
    sender_of = jnp.zeros((1, 256), jnp.int32)
    for k in range(REACH):
        sender_of = jnp.where(
            sort_lane[:1] // 64 == k, sender[:, k : k + 1], sender_of
        )
    same = (sort_row // 64 == sender_of) & (sort_row % 64 == sort_lane % 64)
    sort = jnp.where(same, 1.0, 0.0).astype(BF)

    loads[7].wait()

    @pl.loop(0, feats // 256)
    def _(i):
        cols = pl.ds(pl.multiple_of(i * 256, 256), 256)
        pick = jnp.where(pick_row == 4 * i + pick_lane, 1.0, 0.0).astype(BF)
        bits = jnp.dot(down_bits, pick, preferred_element_type=F32)
        blocks = []
        for k in range(REACH):
            row = jnp.broadcast_to(bits[k : k + 1], (16, 256)).astype(BF)
            block = wd[k * 64 : (k + 1) * 64, cols].reshape(4, 16, 256) * row[None]
            blocks.append(block.reshape(64, 256))
        wdp[:, cols] = jnp.dot(
            sort, jnp.concatenate(blocks, axis=0), preferred_element_type=F32
        ).astype(BF)

    for one in so_copies:
        one.wait_recv()
    row_of = lax.broadcasted_iota(jnp.int32, (256, 128), 0)
    lane_of = lax.broadcasted_iota(jnp.int32, (256, 128), 1)
    for j in range(REACH):
        order = so_v[j]
        mine = jnp.sum(
            jnp.where(order // 4 == t, order % 4, 0), axis=1, keepdims=True
        )
        hit = (row_of == mine * 64 + lane_of % 64) & (lane_of // 64 == j % 2)
        perm[:, j * 128 : (j + 1) * 128] = jnp.where(hit, 1.0, 0.0).astype(BF)

    @pl.when(s > 0)
    def _():
        rows_in = arrive()
        xbuf[0, 0, c] = rows_in
        out_ref[...] = rows_in
        send_own()

    def block_product(d, state):
        gate, upper, squares = state
        for dy in range(ny):
            at = pos(y + ny - dy, z + nz - d)
            wide = jnp.concatenate(
                [xbuf[dy, d, 0], xbuf[dy, d, 1]], axis=1
            ).astype(F32)
            squares = squares + wide * wide
            where = pl.ds(pl.multiple_of(at * 256, 256), 256)
            left = (wide * gain[:, where]).astype(BF)
            gate = gate + jnp.dot(left, wg[where, :], preferred_element_type=F32)
            upper = upper + jnp.dot(left, wu[where, :], preferred_element_type=F32)
        return gate, upper, squares

    state = tuple(jnp.zeros((rows, 256), F32) for _ in range(3))
    for step in range(nz + 2):
        if 1 <= step < nz:
            d = near[step]
            z_gather(d).wait_recv()
            for dy in y_far:
                y_gather(dy, d).start()
            p_gather(0, d).start()
        if 1 <= step <= nz:
            d = near[step - 1]
            for dy in y_far[::-1]:
                y_gather(dy, d).wait_recv()
                p_gather(dy, d).start()
        if step >= 2:
            d = near[step - 2]
            for dy in range(ny):
                remote(
                    xbuf.at[dy, d, c],
                    xbuf.at[dy, d, 1 - c],
                    ap_ss.at[dy, d],
                    ap_rs.at[dy, d],
                    s,
                    partner,
                ).wait_recv()
            state = block_product(d, state)
    gate, upper, squares = state
    scale = lax.rsqrt(jnp.sum(squares, axis=1, keepdims=True) / feats + 1e-05)
    gate = gate * scale
    hidden = (gate / (1.0 + jnp.exp(-gate)) * (upper * scale)).astype(BF)
    routed = jnp.dot(hidden, perm[...], preferred_element_type=F32).astype(BF)

    def hand_over(j):
        return remote(
            hsend.at[j], hrecv.at[j], h_ss.at[j], h_rs.at[j], s, (t + nt - j) % nt
        )

    for j in range(REACH - 1, 0, -1):
        hsend[j] = routed[:, j * 128 : (j + 1) * 128]
        hand_over(j).start()
    for j in range(1, REACH):
        hand_over(j).wait_recv()
    tiles = jnp.concatenate(
        [routed[:, :128] + hrecv[1], hrecv[2] + hrecv[3]], axis=1
    )

    def p_scatter(g):
        some = pl.ds(g * GROUP, GROUP)
        return remote(
            psend.at[some], precv.at[some], p_ss.at[g], p_rs.at[g], s, partner
        )

    def y_scatter(dy, g):
        some = pl.ds(g * GROUP, GROUP)
        return remote(
            ysend.at[dy, some],
            yrecv.at[dy, some],
            y_ss.at[dy, g],
            y_rs.at[dy, g],
            s,
            tp_of(y + dy, z, c),
        )

    for g in range(groups):
        for p in range(g * GROUP, (g + 1) * GROUP):
            for dy in range(ny):
                at = pos(y + dy, z + far[p])
                cols = pl.ds(pl.multiple_of(at * 256, 256), 256)
                both = jnp.dot(tiles, wdp[:, cols], preferred_element_type=F32)
                low, high = both[:, :128], both[:, 128:]
                part[p, dy] = jnp.where(c == 0, low, high)
                psend[p, dy] = jnp.where(c == 0, high, low).astype(BF)
        p_scatter(g).start()
    for g in range(groups):
        p_scatter(g).wait_recv()
        for dy in y_far:
            for p in range(g * GROUP, (g + 1) * GROUP):
                ysend[dy, p] = (part[p, dy] + precv[p, dy].astype(F32)).astype(BF)
            y_scatter(dy, g).start()
    for g in range(groups):
        for dy in y_far[::-1]:
            y_scatter(dy, g).wait_recv()
        for p in range(g * GROUP, (g + 1) * GROUP):
            total = part[p, 0] + precv[p, 0].astype(F32)
            for dy in range(1, ny):
                total = total + yrecv[dy, p].astype(F32)
            zsend[p] = total.astype(BF)
            z_scatter(p).start()

    @pl.when(s == 0)
    def _():
        out_ref[...] = arrive()

    for one in so_copies:
        one.wait_send()
    keep_copy.wait_send()
    for d in range(1, nz):
        z_gather(d).wait_send()
    for d in range(nz):
        for dy in range(1, ny):
            y_gather(dy, d).wait_send()
        for dy in range(ny):
            p_gather(dy, d).wait_send()
        z_scatter(d).wait_send()
    for j in range(1, REACH):
        hand_over(j).wait_send()
    for g in range(groups):
        p_scatter(g).wait_send()
        for dy in range(1, ny):
            y_scatter(dy, g).wait_send()


def body(
    tokens,
    norm_gain,
    gate_weight,
    up_weight,
    gate_mask,
    up_mask,
    down_weight,
    down_mask,
    slot_order,
):
    sections = lax.axis_size("section")
    nt = lax.axis_size("tp")
    ny, nz = tp_grid(nt)
    rows = tokens.shape[0]
    feats = nt * 128
    groups = nz // GROUP
    dma = pltpu.SemaphoreType.DMA
    scratch = [
        pltpu.VMEM((feats, 256), BF),
        pltpu.VMEM((feats, 256), BF),
        pltpu.VMEM((256, feats), BF),
        pltpu.VMEM((256, feats), BF),
        pltpu.VMEM((1, feats), F32),
        pltpu.VMEM((4, feats // 64), jnp.int32),
        pltpu.VMEM((4, feats // 64), jnp.int32),
        pltpu.VMEM((4, feats // 64), jnp.int32),
        pltpu.VMEM((REACH, 1, 4), jnp.int32),
        pltpu.VMEM((feats // 64, 256), F32),
        pltpu.VMEM((feats // 64, 256), F32),
        pltpu.VMEM((256, REACH * 128), BF),
        pltpu.VMEM((ny, nz, 2, rows, 128), BF),
        pltpu.VMEM((rows, 128), BF),
        pltpu.VMEM((REACH, rows, 128), BF),
        pltpu.VMEM((REACH, rows, 128), BF),
        pltpu.VMEM((nz, ny, rows, 128), F32),
        pltpu.VMEM((nz, ny, rows, 128), BF),
        pltpu.VMEM((nz, ny, rows, 128), BF),
        pltpu.VMEM((ny, nz, rows, 128), BF),
        pltpu.VMEM((ny, nz, rows, 128), BF),
        pltpu.VMEM((nz, rows, 128), BF),
        pltpu.VMEM((nz, rows, 128), BF),
        dma((10,)),
    ]
    for shape in (
        (REACH,),
        (nz,),
        (ny, nz),
        (ny, nz),
        (REACH,),
        (groups,),
        (ny, groups),
        (nz,),
        (1,),
    ):
        scratch += [dma(shape), dma(shape)]
    received = pl.pallas_call(
        functools.partial(kernel, sections, ny, nz),
        out_shape=jax.ShapeDtypeStruct((rows, 128), BF),
        in_specs=[pl.BlockSpec(memory_space=pl.ANY)] * 9,
        out_specs=pl.BlockSpec(memory_space=pltpu.VMEM),
        scratch_shapes=scratch,
        compiler_params=pltpu.CompilerParams(
            collective_id=0,
            has_side_effects=True,
            vmem_limit_bytes=50 * 1024 * 1024,
        ),
    )(
        tokens,
        norm_gain,
        gate_weight[0],
        up_weight[0],
        gate_mask[0].T,
        up_mask[0].T,
        down_weight[0],
        down_mask[0],
        slot_order,
    )
    return received[None]


def solution(mesh):
    return jax.shard_map(
        body,
        mesh=mesh,
        in_specs=(
            P(None, "tp"),
            P("section", None),
            P("section", None, "tp"),
            P("section", None, "tp"),
            P("section", None, "tp"),
            P("section", None, "tp"),
            P("section", "tp", None),
            P("section", "tp", None),
            P("section", "tp"),
        ),
        out_specs=P("section", None, "tp"),
        check_vma=False,
    )
```

time: 1130 us -> 178 us (0.16)
  waiting for transfers between devices: 976 us -> 0 us
  Pallas kernels: 0 us -> 173 us
  matrix products: 40.5 us -> 0 us
  starting transfers between devices: 37.1 us -> 0 us
  other arithmetic: 25.9 us -> 0 us
  between operations: 21.4 us -> 0.02 us
  local copies, waits for them, and re-layouts: 25.1 us -> 4.78 us
    reduce_scatter x4 -> x0, waiting for transfers between devices: 527 us -> none  [body(): lax.psum_scatter(partial_sum, 'tp', scatter_dimension=1, tiled=True)]
    all_gather x5 -> x0, waiting for transfers between devices: 341 us -> none  [the longest x4 302 us: body(): section_full = lax.all_gather(y_own, 'tp', axis=1, tiled=True)]
    pallas_call x0 -> x1, Pallas kernels: none -> 173 us  [body(): pl.pallas_call(functools.partial(kernel, sections, ny, nz), out_shape=jax...]
    ppermute x19 -> x0, waiting for transfers between devices: 108 us -> none  [passed_along(): return lax.ppermute(block, axis, route)]
    dot_general x12 -> x0, matrix products: 40.5 us -> none  [the longest x4 19.6 us: body(): partial_sum = jnp.dot(mine, w_down, preferred_element_type=jnp.float32)]
    ppermute x19 -> x0, starting transfers between devices: 36.8 us -> none  [passed_along(): return lax.ppermute(block, axis, route)]
    unnamed x25 -> x13, local copies, waits for them, and re-layouts: 19.2 us -> 4.78 us
    mul x3 -> x0, other arithmetic: 11.4 us -> none  [masked(): return weight * expand_mask(mask, width).astype(jnp.bfloat16)]
  transfers between devices with their start and end apart: 28 -> 0, of which waited for: 16 -> 0; matrix products, arithmetic and copies ran while one was open for 3% -> 0% of each run, Pallas kernels for 0% -> 0%
where the time goes in v1:
time: 178 us
  Pallas kernels  173 us (97%)
  local copies, waits for them, and re-layouts  4.78 us (3%)
    pallas_call x1, Pallas kernels, body(): pl.pallas_call(functools.partial(kernel, sections, ny, nz), out_shape=jax...  173 us
    unnamed x13, local copies, waits for them, and re-layouts  4.78 us

profile of v1, /device:TPU:1, one launch (start us, length us, event | category | flops | bytes accessed | tf_op | source)
XLA Modules:
  0.0 177.8 jit_solution(193155906289875713)
XLA Ops:
  0.0 0.0 copy-start
  0.0 0.8 copy-done
  0.8 0.0 copy-start.1
  0.8 0.7 copy-done.1
  1.5 0.0 copy-start.2
  1.5 0.7 copy-done.2
  2.2 0.0 copy-start.3
  2.2 0.7 copy-done.3
  2.8 0.0 copy-start.4
  2.8 0.7 copy-done.4
  3.5 0.0 copy-start.5
  3.5 0.7 copy-done.5
  4.2 173.0 %shard_map.91 = bf16[64,128]{1,0:T(8,128)(2,1)S(1)} custom-call(bf16[64,128]{1,0:T(8,128)(2,1)S(1)} %copy-done.1, f32[1,8192]{1,0:T(1,128)S(1)} %copy-done, bf16[8192,256]{1,0:T(8,128)(2,1)} %bitcast.15, bf16[8192,256]{1,0:T(8,128)(2,1)} %bitcast.16, s32[4,128]{1,0:T(4,128)S(1)} %bitcast.12, s32[4,128]{1,0:T(4,128)S(1)} %bitcast.13, ...), custom_call_target="tpu_custom_call" | custom-call | tf_op jit(solution)/shard_map/pallas_call | solution.py:471
  177.2 0.6 copy.11
Async XLA Ops:
  0.0 0.8 copy-start
  0.8 0.7 copy-start.1
  1.5 0.7 copy-start.2
  2.2 0.7 copy-start.3
  2.8 0.7 copy-start.4
  3.5 0.7 copy-start.5

commit v2 on v1

--- a/solution.py
+++ b/solution.py
@@ -11,7 +11,7 @@
 BF = jnp.bfloat16
 F32 = jnp.float32
 REACH = 4
-GROUP = 4
+GROUP = 2
 
 
 def tp_grid(count):
@@ -143,76 +143,9 @@
     peers += [(s_last, tp_of(y, z + d, c)) for d in range(nz)]
     for peer in peers:
         pl.semaphore_signal(barrier, inc=1, device_id=peer, device_id_type=MESH)
-    pl.semaphore_wait(barrier, len(peers))
 
     for one in loads[:5]:
         one.wait()
-    so_copies = [
-        remote(so_v.at[0], so_v.at[j], so_ss.at[j], so_rs.at[j], s, (t + j) % nt)
-        for j in range(1, REACH)
-    ]
-    for one in so_copies:
-        one.start()
-
-    own = xbuf.at[0, 0, c]
-
-    def z_gather(d):
-        return remote(
-            own, xbuf.at[0, d, c], az_ss.at[d], az_rs.at[d], s, tp_of(y, z + d, c)
-        )
-
-    def y_gather(dy, d):
-        return remote(
-            xbuf.at[0, d, c],
-            xbuf.at[dy, d, c],
-            ay_ss.at[dy, d],
-            ay_rs.at[dy, d],
-            s,
-            tp_of(y + dy, z, c),
-        )
-
-    def p_gather(dy, d):
-        return remote(
-            xbuf.at[dy, d, c],
-            xbuf.at[dy, d, c],
-            ap_ss.at[dy, d],
-            ap_rs.at[dy, d],
-            s,
-            partner,
-        )
-
-    keep_copy = remote(own, xprev, x_ss.at[0], x_rs.at[0], s_next, t)
-
-    def z_scatter(p):
-        return remote(
-            zsend.at[p],
-            zrecv.at[p],
-            z_ss.at[p],
-            z_rs.at[p],
-            s_next,
-            tp_of(y, z + far[p], c),
-        )
-
-    def send_own():
-        for d in far[:-1]:
-            z_gather(d).start()
-        for dy in y_far:
-            y_gather(dy, 0).start()
-        p_gather(0, 0).start()
-        keep_copy.start()
-
-    def arrive():
-        keep_copy.wait_recv()
-        total = xprev[...].astype(F32)
-        for p in range(nz):
-            z_scatter(p).wait_recv()
-            total = total + zrecv[p].astype(F32)
-        return total.astype(BF)
-
-    @pl.when(s == 0)
-    def _():
-        token_load.wait()
-        send_own()
 
     spread_at = lax.broadcasted_iota(jnp.int32, (4, 256), 1) // 64
     spread_of = lax.broadcasted_iota(jnp.int32, (4, 256), 0)
@@ -226,7 +159,7 @@
         )
 
     def mask_up(weight, wide):
-        @pl.loop(0, feats // 64)
+        @pl.loop(0, feats // 64, unroll=8)
         def _(i):
             at = pl.ds(pl.multiple_of(i * 64, 64), 64)
             row = jnp.broadcast_to(wide[pl.ds(i, 1), :], (16, 256)).astype(BF)
@@ -252,21 +185,97 @@
     same = (sort_row // 64 == sender_of) & (sort_row % 64 == sort_lane % 64)
     sort = jnp.where(same, 1.0, 0.0).astype(BF)
 
+    def mask_down(first, last):
+        @pl.loop(first, last, unroll=2)
+        def _(i):
+            cols = pl.ds(pl.multiple_of(i * 256, 256), 256)
+            pick = jnp.where(pick_row == 4 * i + pick_lane, 1.0, 0.0).astype(BF)
+            bits = jnp.dot(down_bits, pick, preferred_element_type=F32)
+            blocks = []
+            for k in range(REACH):
+                row = jnp.broadcast_to(bits[k : k + 1], (16, 256)).astype(BF)
+                block = wd[k * 64 : (k + 1) * 64, cols]
+                block = block.reshape(4, 16, 256) * row[None]
+                blocks.append(block.reshape(64, 256))
+            wdp[:, cols] = jnp.dot(
+                sort, jnp.concatenate(blocks, axis=0), preferred_element_type=F32
+            ).astype(BF)
+
+    tiles_down = feats // 256
+    early, middle = tiles_down * 3 // 16 * 2, tiles_down * 5 // 16 * 2
     loads[7].wait()
-
-    @pl.loop(0, feats // 256)
-    def _(i):
-        cols = pl.ds(pl.multiple_of(i * 256, 256), 256)
-        pick = jnp.where(pick_row == 4 * i + pick_lane, 1.0, 0.0).astype(BF)
-        bits = jnp.dot(down_bits, pick, preferred_element_type=F32)
-        blocks = []
-        for k in range(REACH):
-            row = jnp.broadcast_to(bits[k : k + 1], (16, 256)).astype(BF)
-            block = wd[k * 64 : (k + 1) * 64, cols].reshape(4, 16, 256) * row[None]
-            blocks.append(block.reshape(64, 256))
-        wdp[:, cols] = jnp.dot(
-            sort, jnp.concatenate(blocks, axis=0), preferred_element_type=F32
-        ).astype(BF)
+    mask_down(0, early)
+
+    pl.semaphore_wait(barrier, len(peers))
+
+    own = xbuf.at[0, 0, c]
+
+    def z_gather(d):
+        return remote(
+            own, xbuf.at[0, d, c], az_ss.at[d], az_rs.at[d], s, tp_of(y, z + d, c)
+        )
+
+    def y_gather(dy, d):
+        return remote(
+            xbuf.at[0, d, c],
+            xbuf.at[dy, d, c],
+            ay_ss.at[dy, d],
+            ay_rs.at[dy, d],
+            s,
+            tp_of(y + dy, z, c),
+        )
+
+    def p_gather(dy, d):
+        return remote(
+            xbuf.at[dy, d, c],
+            xbuf.at[dy, d, c],
+            ap_ss.at[dy, d],
+            ap_rs.at[dy, d],
+            s,
+            partner,
+        )
+
+    keep_copy = remote(own, xprev, x_ss.at[0], x_rs.at[0], s_next, t)
+
+    def z_scatter(p):
+        return remote(
+            zsend.at[p],
+            zrecv.at[p],
+            z_ss.at[p],
+            z_rs.at[p],
+            s_next,
+            tp_of(y, z + far[p], c),
+        )
+
+    def send_own():
+        for d in far[:-1]:
+            z_gather(d).start()
+        for dy in y_far:
+            y_gather(dy, 0).start()
+        p_gather(0, 0).start()
+        keep_copy.start()
+
+    def arrive():
+        keep_copy.wait_recv()
+        total = xprev[...].astype(F32)
+        for p in range(nz):
+            z_scatter(p).wait_recv()
+            total = total + zrecv[p].astype(F32)
+        return total.astype(BF)
+
+    @pl.when(s == 0)
+    def _():
+        token_load.wait()
+        send_own()
+
+    so_copies = [
+        remote(so_v.at[0], so_v.at[j], so_ss.at[j], so_rs.at[j], s, (t + j) % nt)
+        for j in range(1, REACH)
+    ]
+    for one in so_copies:
+        one.start()
+
+    mask_down(early, middle)
 
     for one in so_copies:
         one.wait_recv()
@@ -282,6 +291,7 @@
 
     @pl.when(s > 0)
     def _():
+        mask_down(middle, tiles_down)
         rows_in = arrive()
         xbuf[0, 0, c] = rows_in
         out_ref[...] = rows_in
@@ -302,20 +312,24 @@
         return gate, upper, squares
 
     state = tuple(jnp.zeros((rows, 256), F32) for _ in range(3))
-    for step in range(nz + 2):
-        if 1 <= step < nz:
+    for d in near[1:]:
+        z_gather(d).wait_recv()
+        for dy in y_far:
+            y_gather(dy, d).start()
+        p_gather(0, d).start()
+
+    @pl.when(s == 0)
+    def _():
+        mask_down(middle, tiles_down)
+
+    for step in range(nz + 1):
+        if step < nz:
             d = near[step]
-            z_gather(d).wait_recv()
-            for dy in y_far:
-                y_gather(dy, d).start()
-            p_gather(0, d).start()
-        if 1 <= step <= nz:
-            d = near[step - 1]
             for dy in y_far[::-1]:
                 y_gather(dy, d).wait_recv()
                 p_gather(dy, d).start()
-        if step >= 2:
-            d = near[step - 2]
+        if step >= 1:
+            d = near[step - 1]
             for dy in range(ny):
                 remote(
                     xbuf.at[dy, d, c],
@@ -477,7 +491,7 @@
         compiler_params=pltpu.CompilerParams(
             collective_id=0,
             has_side_effects=True,
-            vmem_limit_bytes=50 * 1024 * 1024,
+            vmem_limit_bytes=67043328,
         ),
     )(
         tokens,

time: 178 us -> 138 us (0.78)
  Pallas kernels: 173 us -> 136 us
  local copies, waits for them, and re-layouts: 4.78 us -> 1.32 us
    pallas_call x1, Pallas kernels: 173 us -> 136 us  [body(): pl.pallas_call(functools.partial(kernel, sections, ny, nz), out_shape=jax...]
    unnamed x13 -> x1, local copies, waits for them, and re-layouts: 4.78 us -> 1.32 us
where the time goes in v2:
time: 138 us; the launch traced here: 137 us
  Pallas kernels  136 us (99%)
    pallas_call x1, Pallas kernels, body(): pl.pallas_call(functools.partial(kernel, sections, ny, nz), out_shape=jax...  136 us

profile of v2, /device:TPU:1, one launch (start us, length us, event | category | flops | bytes accessed | tf_op | source)
XLA Modules:
  0.0 137.4 jit_solution(17830050232495262190)
XLA Ops:
  0.0 136.1 %shard_map.91 = bf16[64,128]{1,0:T(8,128)(2,1)} custom-call(bf16[64,128]{1,0:T(8,128)(2,1)} %tokens_h.1, f32[1,8192]{1,0:T(1,128)} %gain_h.1, bf16[8192,256]{1,0:T(8,128)(2,1)} %bitcast.11, bf16[8192,256]{1,0:T(8,128)(2,1)} %bitcast.12, s32[4,128]{1,0:T(4,128)} %bitcast.15, s32[4,128]{1,0:T(4,128)} %bitcast.16, bf16[256,8192]{1,0:T(8,128)(2,1)} %bitcast.13, ...), custom_call_target="tpu_custom_call" | custom-call | tf_op jit(solution)/shard_map/pallas_call | solution.py:485
  136.1 1.3 copy.11

commit v3 on v2

--- a/solution.py
+++ b/solution.py
@@ -12,6 +12,8 @@
 F32 = jnp.float32
 REACH = 4
 GROUP = 2
+ACROSS = (1,)
+MOVE_FROM = 3
 
 
 def tp_grid(count):
@@ -44,6 +46,7 @@
     so_v,
     gme,
     ume,
+    dme,
     perm,
     xbuf,
     xprev,
@@ -75,6 +78,8 @@
     z_rs,
     x_ss,
     x_rs,
+    m_ss,
+    m_rs,
 ):
     nt = ny * nz * 2
     rows = tokens_h.shape[0]
@@ -141,6 +146,8 @@
     peers += [(s, (t + nt - d) % nt) for d in range(1, REACH)]
     peers += [(s_next, tp_of(y, z + d, c)) for d in range(nz)]
     peers += [(s_last, tp_of(y, z + d, c)) for d in range(nz)]
+    peers += [(s_next, tp_of(y + d, z, c)) for d in range(1, ny)]
+    peers += [(s_last, tp_of(y + d, z, c)) for d in range(1, ny)]
     for peer in peers:
         pl.semaphore_signal(barrier, inc=1, device_id=peer, device_id_type=MESH)
 
@@ -172,8 +179,24 @@
     mask_up(wu, ume)
 
     down_bits = dm[...].astype(BF)
-    pick_row = lax.broadcasted_iota(jnp.int32, (feats // 64, 256), 0)
-    pick_lane = lax.broadcasted_iota(jnp.int32, (feats // 64, 256), 1) // 64
+    entries = feats // 64
+    pick_row = lax.broadcasted_iota(jnp.int32, (entries, entries), 0)
+    pick_lane = lax.broadcasted_iota(jnp.int32, (entries, entries), 1)
+    row_is = lax.broadcasted_iota(jnp.int32, (4, entries), 0)
+    lane_is = lax.broadcasted_iota(jnp.int32, (4, entries), 1)
+    turned = jnp.zeros((4, entries), F32)
+    for q in range(4):
+        pick = jnp.where(pick_row == pick_lane // 4 * 4 + q, 1.0, 0.0).astype(BF)
+        found = jnp.dot(down_bits, pick, preferred_element_type=F32)
+        found = jnp.where(row_is == lane_is % 4, found, 0.0)
+        found = jnp.sum(found, axis=0, keepdims=True)
+        turned = turned + jnp.where(row_is == q, found, 0.0)
+    dme[...] = lax.dot_general(
+        turned.astype(BF),
+        spread,
+        (((0,), (0,)), ((), ())),
+        preferred_element_type=F32,
+    )
     sort_row = lax.broadcasted_iota(jnp.int32, (256, 256), 0)
     sort_lane = lax.broadcasted_iota(jnp.int32, (256, 256), 1)
     sender = (so_v[0] // 4 + nt - t) % nt
@@ -189,15 +212,14 @@
         @pl.loop(first, last, unroll=2)
         def _(i):
             cols = pl.ds(pl.multiple_of(i * 256, 256), 256)
-            pick = jnp.where(pick_row == 4 * i + pick_lane, 1.0, 0.0).astype(BF)
-            bits = jnp.dot(down_bits, pick, preferred_element_type=F32)
             blocks = []
             for k in range(REACH):
-                row = jnp.broadcast_to(bits[k : k + 1], (16, 256)).astype(BF)
+                row = dme[pl.ds(4 * i + k, 1), :]
+                row = jnp.broadcast_to(row, (16, 256)).astype(BF)
                 block = wd[k * 64 : (k + 1) * 64, cols]
                 block = block.reshape(4, 16, 256) * row[None]
                 blocks.append(block.reshape(64, 256))
-            wdp[:, cols] = jnp.dot(
+            wdp[0, :, cols] = jnp.dot(
                 sort, jnp.concatenate(blocks, axis=0), preferred_element_type=F32
             ).astype(BF)
 
@@ -243,8 +265,19 @@
             zrecv.at[p],
             z_ss.at[p],
             z_rs.at[p],
-            s_next,
+            s if p // GROUP in ACROSS else s_next,
             tp_of(y, z + far[p], c),
+        )
+
+    def y_scatter(dy, g):
+        some = pl.ds(g * GROUP, GROUP)
+        return remote(
+            ysend.at[dy, some],
+            yrecv.at[dy, some],
+            y_ss.at[dy, g],
+            y_rs.at[dy, g],
+            s_next if g in ACROSS else s,
+            tp_of(y + dy, z, c),
         )
 
     def send_own():
@@ -256,6 +289,15 @@
         keep_copy.start()
 
     def arrive():
+        for g in ACROSS:
+            for dy in range(ny):
+                y_scatter(dy, g).wait_recv()
+            for p in range(g * GROUP, (g + 1) * GROUP):
+                total = yrecv[0, p].astype(F32)
+                for dy in range(1, ny):
+                    total = total + yrecv[dy, p].astype(F32)
+                zsend[p] = total.astype(BF)
+                z_scatter(p).start()
         keep_copy.wait_recv()
         total = xprev[...].astype(F32)
         for p in range(nz):
@@ -289,9 +331,37 @@
         hit = (row_of == mine * 64 + lane_of % 64) & (lane_of // 64 == j % 2)
         perm[:, j * 128 : (j + 1) * 128] = jnp.where(hit, 1.0, 0.0).astype(BF)
 
+    def move(j):
+        block = pl.ds(j * 64, 64)
+        return remote(
+            wdp.at[0, block],
+            wdp.at[1, block],
+            m_ss.at[j],
+            m_rs.at[j],
+            s,
+            (t + j) % nt,
+        )
+
+    moved = jnp.where(s >= MOVE_FROM, 1, 0)
+
     @pl.when(s > 0)
     def _():
         mask_down(middle, tiles_down)
+
+    @pl.when(s >= MOVE_FROM)
+    def _():
+        for j in range(1, REACH):
+            move(j).start()
+        stay = pltpu.make_async_copy(
+            wdp.at[0, pl.ds(0, 64)], wdp.at[1, pl.ds(0, 64)], m_rs.at[0]
+        )
+        stay.start()
+        for j in range(1, REACH):
+            move(j).wait()
+        stay.wait()
+
+    @pl.when(s > 0)
+    def _():
         rows_in = arrive()
         xbuf[0, 0, c] = rows_in
         out_ref[...] = rows_in
@@ -351,11 +421,19 @@
             hsend.at[j], hrecv.at[j], h_ss.at[j], h_rs.at[j], s, (t + nt - j) % nt
         )
 
-    for j in range(REACH - 1, 0, -1):
-        hsend[j] = routed[:, j * 128 : (j + 1) * 128]
-        hand_over(j).start()
-    for j in range(1, REACH):
-        hand_over(j).wait_recv()
+    @pl.when(s < MOVE_FROM)
+    def _():
+        for j in range(REACH - 1, 0, -1):
+            hsend[j] = routed[:, j * 128 : (j + 1) * 128]
+            hand_over(j).start()
+        for j in range(1, REACH):
+            hand_over(j).wait()
+
+    @pl.when(s >= MOVE_FROM)
+    def _():
+        for j in range(1, REACH):
+            hrecv[j] = routed[:, j * 128 : (j + 1) * 128]
+
     tiles = jnp.concatenate(
         [routed[:, :128] + hrecv[1], hrecv[2] + hrecv[3]], axis=1
     )
@@ -364,17 +442,6 @@
         some = pl.ds(g * GROUP, GROUP)
         return remote(
             psend.at[some], precv.at[some], p_ss.at[g], p_rs.at[g], s, partner
-        )
-
-    def y_scatter(dy, g):
-        some = pl.ds(g * GROUP, GROUP)
-        return remote(
-            ysend.at[dy, some],
-            yrecv.at[dy, some],
-            y_ss.at[dy, g],
-            y_rs.at[dy, g],
-            s,
-            tp_of(y + dy, z, c),
         )
 
     for g in range(groups):
@@ -382,18 +449,20 @@
             for dy in range(ny):
                 at = pos(y + dy, z + far[p])
                 cols = pl.ds(pl.multiple_of(at * 256, 256), 256)
-                both = jnp.dot(tiles, wdp[:, cols], preferred_element_type=F32)
+                both = jnp.dot(tiles, wdp[moved, :, cols], preferred_element_type=F32)
                 low, high = both[:, :128], both[:, 128:]
                 part[p, dy] = jnp.where(c == 0, low, high)
                 psend[p, dy] = jnp.where(c == 0, high, low).astype(BF)
         p_scatter(g).start()
     for g in range(groups):
         p_scatter(g).wait_recv()
-        for dy in y_far:
+        for dy in y_far + ([0] if g in ACROSS else []):
             for p in range(g * GROUP, (g + 1) * GROUP):
                 ysend[dy, p] = (part[p, dy] + precv[p, dy].astype(F32)).astype(BF)
             y_scatter(dy, g).start()
     for g in range(groups):
+        if g in ACROSS:
+            continue
         for dy in y_far[::-1]:
             y_scatter(dy, g).wait_recv()
         for p in range(g * GROUP, (g + 1) * GROUP):
@@ -418,11 +487,9 @@
         for dy in range(ny):
             p_gather(dy, d).wait_send()
         z_scatter(d).wait_send()
-    for j in range(1, REACH):
-        hand_over(j).wait_send()
     for g in range(groups):
         p_scatter(g).wait_send()
-        for dy in range(1, ny):
+        for dy in range(0 if g in ACROSS else 1, ny):
             y_scatter(dy, g).wait_send()
 
 
@@ -448,12 +515,13 @@
         pltpu.VMEM((feats, 256), BF),
         pltpu.VMEM((feats, 256), BF),
         pltpu.VMEM((256, feats), BF),
-        pltpu.VMEM((256, feats), BF),
+        pltpu.VMEM((2, 256, feats), BF),
         pltpu.VMEM((1, feats), F32),
         pltpu.VMEM((4, feats // 64), jnp.int32),
         pltpu.VMEM((4, feats // 64), jnp.int32),
         pltpu.VMEM((4, feats // 64), jnp.int32),
         pltpu.VMEM((REACH, 1, 4), jnp.int32),
+        pltpu.VMEM((feats // 64, 256), F32),
         pltpu.VMEM((feats // 64, 256), F32),
         pltpu.VMEM((feats // 64, 256), F32),
         pltpu.VMEM((256, REACH * 128), BF),
@@ -480,6 +548,7 @@
         (ny, groups),
         (nz,),
         (1,),
+        (REACH,),
     ):
         scratch += [dma(shape), dma(shape)]
     received = pl.pallas_call(

time: 138 us -> 127 us (0.920)
  Pallas kernels: 136 us -> 126 us
    pallas_call x1, Pallas kernels: 136 us -> 126 us  [body(): pl.pallas_call(functools.partial(kernel, sections, ny, nz), out_shape=jax...]
where the time goes in v3:
time: 127 us
  Pallas kernels  126 us (99%)
  local copies, waits for them, and re-layouts  1.32 us (1%)
    pallas_call x1, Pallas kernels, body(): pl.pallas_call(functools.partial(kernel, sections, ny, nz), out_shape=jax...  126 us

profile of v3, /device:TPU:1, one launch (start us, length us, event | category | flops | bytes accessed | tf_op | source)
XLA Modules:
  0.0 127.3 jit_solution(8213219881691789615)
XLA Ops:
  0.0 125.9 %shard_map.91 = bf16[64,128]{1,0:T(8,128)(2,1)} custom-call(bf16[64,128]{1,0:T(8,128)(2,1)} %tokens_h.1, f32[1,8192]{1,0:T(1,128)} %gain_h.1, bf16[8192,256]{1,0:T(8,128)(2,1)} %bitcast.11, bf16[8192,256]{1,0:T(8,128)(2,1)} %bitcast.12, s32[4,128]{1,0:T(4,128)} %bitcast.15, s32[4,128]{1,0:T(4,128)} %bitcast.16, bf16[256,8192]{1,0:T(8,128)(2,1)} %bitcast.13, ...), custom_call_target="tpu_custom_call" | custom-call | tf_op jit(solution)/shard_map/pallas_call | solution.py:554
  125.9 1.3 %copy.11 = bf16[1,64,128]{2,1,0:T(8,128)(2,1)} copy(bf16[1,64,128]{2,1,0:T(8,128)(2,1)} %bitcast.14) | data formatting | bytes 32768

commit v4 on v3

--- a/solution.py
+++ b/solution.py
@@ -209,7 +209,7 @@
     sort = jnp.where(same, 1.0, 0.0).astype(BF)
 
     def mask_down(first, last):
-        @pl.loop(first, last, unroll=2)
+        @pl.loop(first, last, unroll=4)
         def _(i):
             cols = pl.ds(pl.multiple_of(i * 256, 256), 256)
             blocks = []
@@ -224,7 +224,7 @@
             ).astype(BF)
 
     tiles_down = feats // 256
-    early, middle = tiles_down * 3 // 16 * 2, tiles_down * 5 // 16 * 2
+    early, middle = tiles_down // 4, tiles_down // 2
     loads[7].wait()
     mask_down(0, early)
 

time: 127 us -> 128 us (level)
  no operation moved by 1% of the time
where the time goes in v4:
time: 128 us
  Pallas kernels  126 us (98%)
  local copies, waits for them, and re-layouts  1.32 us (1%)
    pallas_call x1, Pallas kernels, body(): pl.pallas_call(functools.partial(kernel, sections, ny, nz), out_shape=jax...  126 us

profile of v4, /device:TPU:1, one launch (start us, length us, event | category | flops | bytes accessed | tf_op | source)
XLA Modules:
  0.0 127.6 jit_solution(3745492589377488456)
XLA Ops:
  0.0 126.3 %shard_map.91 = bf16[64,128]{1,0:T(8,128)(2,1)} custom-call(bf16[64,128]{1,0:T(8,128)(2,1)} %tokens_h.1, f32[1,8192]{1,0:T(1,128)} %gain_h.1, bf16[8192,256]{1,0:T(8,128)(2,1)} %bitcast.11, bf16[8192,256]{1,0:T(8,128)(2,1)} %bitcast.12, s32[4,128]{1,0:T(4,128)} %bitcast.15, s32[4,128]{1,0:T(4,128)} %bitcast.16, bf16[256,8192]{1,0:T(8,128)(2,1)} %bitcast.13, ...), custom_call_target="tpu_custom_call" | custom-call | tf_op jit(solution)/shard_map/pallas_call | solution.py:554
  126.3 1.3 %copy.11 = bf16[1,64,128]{2,1,0:T(8,128)(2,1)} copy(bf16[1,64,128]{2,1,0:T(8,128)(2,1)} %bitcast.14) | data formatting | bytes 32768

commit v5 on v3

--- a/solution.py
+++ b/solution.py
@@ -12,6 +12,7 @@
 F32 = jnp.float32
 REACH = 4
 GROUP = 2
+LAG = 2
 ACROSS = (1,)
 MOVE_FROM = 3
 
@@ -444,6 +445,13 @@
             psend.at[some], precv.at[some], p_ss.at[g], p_rs.at[g], s, partner
         )
 
+    def sum_pair(g):
+        p_scatter(g).wait_recv()
+        for dy in y_far + ([0] if g in ACROSS else []):
+            for p in range(g * GROUP, (g + 1) * GROUP):
+                ysend[dy, p] = (part[p, dy] + precv[p, dy].astype(F32)).astype(BF)
+            y_scatter(dy, g).start()
+
     for g in range(groups):
         for p in range(g * GROUP, (g + 1) * GROUP):
             for dy in range(ny):
@@ -454,12 +462,10 @@
                 part[p, dy] = jnp.where(c == 0, low, high)
                 psend[p, dy] = jnp.where(c == 0, high, low).astype(BF)
         p_scatter(g).start()
-    for g in range(groups):
-        p_scatter(g).wait_recv()
-        for dy in y_far + ([0] if g in ACROSS else []):
-            for p in range(g * GROUP, (g + 1) * GROUP):
-                ysend[dy, p] = (part[p, dy] + precv[p, dy].astype(F32)).astype(BF)
-            y_scatter(dy, g).start()
+        if g >= LAG:
+            sum_pair(g - LAG)
+    for g in range(max(groups - LAG, 0), groups):
+        sum_pair(g)
     for g in range(groups):
         if g in ACROSS:
             continue

time: 127 us -> 129 us (1.016)
  no operation moved by 1% of the time
where the time goes in v5:
time: 129 us; the launch traced here: 128 us
  Pallas kernels  127 us (98%)
  local copies, waits for them, and re-layouts  1.32 us (1%)
    pallas_call x1, Pallas kernels, body(): pl.pallas_call(functools.partial(kernel, sections, ny, nz), out_shape=jax...  127 us

profile of v5, /device:TPU:1, one launch (start us, length us, event | category | flops | bytes accessed | tf_op | source)
XLA Modules:
  0.0 128.4 jit_solution(2487126225442540278)
XLA Ops:
  0.0 127.0 %shard_map.91 = bf16[64,128]{1,0:T(8,128)(2,1)} custom-call(bf16[64,128]{1,0:T(8,128)(2,1)} %tokens_h.1, f32[1,8192]{1,0:T(1,128)} %gain_h.1, bf16[8192,256]{1,0:T(8,128)(2,1)} %bitcast.11, bf16[8192,256]{1,0:T(8,128)(2,1)} %bitcast.12, s32[4,128]{1,0:T(4,128)} %bitcast.15, s32[4,128]{1,0:T(4,128)} %bitcast.16, bf16[256,8192]{1,0:T(8,128)(2,1)} %bitcast.13, ...), custom_call_target="tpu_custom_call" | custom-call | tf_op jit(solution)/shard_map/pallas_call | solution.py:560
  127.1 1.3 %copy.11 = bf16[1,64,128]{2,1,0:T(8,128)(2,1)} copy(bf16[1,64,128]{2,1,0:T(8,128)(2,1)} %bitcast.14) | data formatting | bytes 32768
